TPU v7x, 32 devices: a whole 2x2x4 slice. The times are simulated.
32 devices in a mesh: grp: 8 (over z, core), row: 4 (over y, x).
Axes of the slice: x: 2, y: 2, z: 4, core: 2. Of those that a mesh axis runs over, the one named last changes fastest.
Arguments:
- theta: float32 [16, 512, 512], P('grp', 'row'), may hold values from -8 to 8
- left_env: bfloat16 [16, 8, 512, 512], P('grp', None, 'row'), may hold values from -1.5 to 1.5
- right_env: bfloat16 [16, 8, 512, 512], P('grp', None, 'row'), may hold values from -3.5 to 3.5
- lengths: int32 [16, 2], P('grp'), may hold values from 128 to 512
Outputs:
- evolved: float32 [16, 512, 512], P('grp', 'row')
- hessenberg: float32 [8, 8], replicated
All inputs are finite; a program needn't handle non-finite values.
Results may differ from a plain program's by a relative error of at most 0.0029.
Values may be sent and summed in bfloat16 or wider, within the bound.
A program may use at most 64 MiB of HBM per device.

v0:
```python
import jax
import jax.numpy as jnp
from jax import lax
from jax.sharding import PartitionSpec as P

KRYLOV = 8
epsilon = 1e-06
time_step = 0.5


def propagate(hessenberg):
    krylov_size = hessenberg.shape[0]
    scaled = time_step * hessenberg
    series = jnp.eye(krylov_size, dtype=jnp.float32)
    series_term = jnp.eye(krylov_size, dtype=jnp.float32)
    for degree in range(1, 19):
        series_term = jnp.dot(series_term, scaled, precision=lax.Precision.HIGHEST) / degree
        series = series + series_term
    return series[:, 0]


def local(theta, left_env, right_env, lengths):
    local_rows = theta.shape[1]
    sect_width = theta.shape[2]
    row_start = lax.axis_index("row") * local_rows
    row_ids = row_start + lax.broadcasted_iota(jnp.int32, (1, local_rows, 1), 1)
    col_ids = lax.broadcasted_iota(jnp.int32, (1, 1, sect_width), 2)
    live_mask = (
        (row_ids < lengths[:, 0][:, None, None]) & (col_ids < lengths[:, 1][:, None, None])
    ).astype(jnp.float32)
    right_full = lax.all_gather(right_env, "row", axis=2, tiled=True)
    start_block = theta * live_mask
    norm_zero = jnp.sqrt(lax.psum(jnp.sum(start_block * start_block), ("grp", "row")) + epsilon)
    krylov_basis = [start_block / norm_zero]
    krylov_size = KRYLOV
    hessenberg = jnp.zeros((krylov_size, krylov_size), jnp.float32)
    for column in range(krylov_size):
        packed = krylov_basis[column].astype(jnp.bfloat16)
        inner_terms = jnp.einsum(
            "sab,swbc->swac", packed, right_full, preferred_element_type=jnp.float32
        )
        inner_terms = inner_terms.astype(jnp.bfloat16)
        partial_image = jnp.einsum(
            "swba,swbc->sac", left_env, inner_terms, preferred_element_type=jnp.float32
        )
        image = lax.psum_scatter(partial_image, "row", scatter_dimension=1, tiled=True) * live_mask
        local_dots = jnp.stack([jnp.sum(vector * image) for vector in krylov_basis])
        coefficients, squared = lax.psum((local_dots, jnp.sum(image * image)), ("grp", "row"))
        for previous in range(column + 1):
            image = image - coefficients[previous] * krylov_basis[previous]
        hessenberg = hessenberg.at[: column + 1, column].set(coefficients)
        if column + 1 < krylov_size:
            beta_norm = jnp.sqrt(squared - jnp.sum(coefficients * coefficients) + epsilon)
            hessenberg = hessenberg.at[column + 1, column].set(beta_norm)
            krylov_basis.append(image / beta_norm)
    weights = propagate(hessenberg)
    evolved = jnp.zeros_like(start_block)
    for column in range(krylov_size):
        evolved = evolved + weights[column] * krylov_basis[column]
    return (norm_zero * evolved, hessenberg)


def solution(mesh):
    return jax.shard_map(
        local,
        mesh=mesh,
        in_specs=(
            P("grp", "row", None),
            P("grp", None, "row", None),
            P("grp", None, "row", None),
            P("grp", None),
        ),
        out_specs=(P("grp", "row", None), P()),
        check_vma=False,
    )
```

profile of v0, /device:TPU:0, one launch (start us, length us, event | category | flops | bytes accessed | tf_op | source)
XLA Modules:
  0.0 891.1 jit_solution(13568998900987345164)
XLA Ops:
  9.7 42.8 %psum.112 = f32[]{:T(128)} all-reduce(f32[]{:T(128)} %multiply_reduce_fusion.43), channel_id=1, replica_groups=mesh['grp'=8,'row'=4] {'grp','row'}, use_global_device_ids=true, to_apply=%region_1.0 | all-reduce | flops 1 | bytes 8 | tf_op jit(solution)/shard_map/psum | solution.py:33
  53.2 47.2 %all-gather.2.cloned.1.call-done = bf16[2,8,512,512]{3,2,1,0:T(8,128)(2,1)} async-done(((bf16[2,8,128,512]{3,2,1,0:T(8,128)(2,1)}), bf16[2,8,512,512]{3,2,1,0:T(8,128)(2,1)}) %all-gather.2.cloned.1.call-update) | async-done | bytes 8388624 | tf_op jit(solution)/shard_map/all_gather | solution.py:31
  100.4 8.9 fusion.24
  109.3 35.3 %reduce-scatter.9.cloned.1.call-done = f32[2,128,512]{1,2,0:T(8,128)} async-done(((f32[2,512,512]{1,2,0:T(8,128)}), f32[2,128,512]{1,2,0:T(8,128)}) %reduce-scatter.9.cloned.1.call-update) | async-done | bytes 524304 | tf_op jit(solution)/shard_map/reduce_scatter | solution.py:46
  146.5 39.5 %all-reduce.7 = (f32[]{:T(128)}, f32[1]{0:T(128)}) all-reduce(f32[]{:T(128)} %get-tuple-element.226, f32[1]{0:T(128)} %bitcast.6), channel_id=1, replica_groups=mesh['grp'=8,'row'=4] {'grp','row'}, use_global_device_ids=true, to_apply=%region_6.0 | all-reduce | flops 2 | bytes 16 | tf_op jit(solution)/shard_map/psum | solution.py:48
  198.6 36.3 %reduce-scatter.11.cloned.1.call-done = f32[2,128,512]{1,2,0:T(8,128)} async-done(((f32[2,512,512]{1,2,0:T(8,128)}), f32[2,128,512]{1,2,0:T(8,128)}) %reduce-scatter.11.cloned.1.call-update) | async-done | bytes 524304 | tf_op jit(solution)/shard_map/reduce_scatter | solution.py:46
  238.1 39.6 %all-reduce.6 = (f32[]{:T(128)}, f32[2]{0:T(128)S(1)}) all-reduce(f32[]{:T(128)} %get-tuple-element.224, f32[2]{0:T(128)S(1)} %pad_maximum_fusion), channel_id=1, replica_groups=mesh['grp'=8,'row'=4] {'grp','row'}, use_global_device_ids=true, to_apply=%region_12.0 | all-reduce | flops 3 | bytes 24 | tf_op jit(solution)/shard_map/psum | solution.py:48
  283.5 8.9 fusion.34
  292.4 36.2 %reduce-scatter.13.cloned.1.call-done = f32[2,128,512]{1,2,0:T(8,128)} async-done(((f32[2,512,512]{1,2,0:T(8,128)}), f32[2,128,512]{1,2,0:T(8,128)}) %reduce-scatter.13.cloned.1.call-update) | async-done | bytes 524304 | tf_op jit(solution)/shard_map/reduce_scatter | solution.py:46
  332.8 39.5 %all-reduce.5 = (f32[]{:T(128)}, f32[3]{0:T(128)S(1)}) all-reduce(f32[]{:T(128)} %get-tuple-element.221, f32[3]{0:T(128)S(1)} %pad_maximum_fusion.1), channel_id=1, replica_groups=mesh['grp'=8,'row'=4] {'grp','row'}, use_global_device_ids=true, to_apply=%region_21.0 | all-reduce | flops 4 | bytes 32 | tf_op jit(solution)/shard_map/psum | solution.py:48
  378.9 8.9 fusion.39
  387.9 36.3 %reduce-scatter.15.cloned.1.call-done = f32[2,128,512]{1,2,0:T(8,128)} async-done(((f32[2,512,512]{1,2,0:T(8,128)}), f32[2,128,512]{1,2,0:T(8,128)}) %reduce-scatter.15.cloned.1.call-update) | async-done | bytes 524304 | tf_op jit(solution)/shard_map/reduce_scatter | solution.py:46
  429.0 39.7 %all-reduce.4 = (f32[]{:T(128)}, f32[4]{0:T(128)S(1)}) all-reduce(f32[]{:T(128)} %get-tuple-element.217, f32[4]{0:T(128)S(1)} %pad_maximum_fusion.2), channel_id=1, replica_groups=mesh['grp'=8,'row'=4] {'grp','row'}, use_global_device_ids=true, to_apply=%region_31.0 | all-reduce | flops 5 | bytes 40 | tf_op jit(solution)/shard_map/psum | solution.py:48
  476.2 8.9 fusion.44
  485.2 36.2 %reduce-scatter.17.cloned.1.call-done = f32[2,128,512]{1,2,0:T(8,128)} async-done(((f32[2,512,512]{1,2,0:T(8,128)}), f32[2,128,512]{1,2,0:T(8,128)}) %reduce-scatter.17.cloned.1.call-update) | async-done | bytes 524304 | tf_op jit(solution)/shard_map/reduce_scatter | solution.py:46
  527.1 39.5 %all-reduce.3 = (f32[]{:T(128)}, f32[5]{0:T(128)S(1)}) all-reduce(f32[]{:T(128)} %get-tuple-element.211, f32[5]{0:T(128)S(1)} %stack.147), channel_id=1, replica_groups=mesh['grp'=8,'row'=4] {'grp','row'}, use_global_device_ids=true, to_apply=%region_42.0 | all-reduce | flops 6 | bytes 48 | tf_op jit(solution)/shard_map/psum | solution.py:48
  575.1 8.9 fusion.49
  584.0 36.3 %reduce-scatter.19.cloned.1.call-done = f32[2,128,512]{1,2,0:T(8,128)} async-done(((f32[2,512,512]{1,2,0:T(8,128)}), f32[2,128,512]{1,2,0:T(8,128)}) %reduce-scatter.19.cloned.1.call-update) | async-done | bytes 524304 | tf_op jit(solution)/shard_map/reduce_scatter | solution.py:46
  626.9 39.9 %all-reduce.2 = (f32[]{:T(128)}, f32[6]{0:T(128)S(1)}) all-reduce(f32[]{:T(128)} %get-tuple-element.205, f32[6]{0:T(128)S(1)} %stack.154), channel_id=1, replica_groups=mesh['grp'=8,'row'=4] {'grp','row'}, use_global_device_ids=true, to_apply=%region_54.0 | all-reduce | flops 7 | bytes 56 | tf_op jit(solution)/shard_map/psum | solution.py:48
  676.0 8.9 fusion.54
  684.9 36.3 %reduce-scatter.21.cloned.1.call-done = f32[2,128,512]{1,2,0:T(8,128)} async-done(((f32[2,512,512]{1,2,0:T(8,128)}), f32[2,128,512]{1,2,0:T(8,128)}) %reduce-scatter.21.cloned.1.call-update) | async-done | bytes 524304 | tf_op jit(solution)/shard_map/reduce_scatter | solution.py:46
  728.7 39.5 %all-reduce.1 = (f32[]{:T(128)}, f32[7]{0:T(128)S(1)}) all-reduce(f32[]{:T(128)} %get-tuple-element.198, f32[7]{0:T(128)S(1)} %stack.162), channel_id=1, replica_groups=mesh['grp'=8,'row'=4] {'grp','row'}, use_global_device_ids=true, to_apply=%region_67.0 | all-reduce | flops 8 | bytes 64 | tf_op jit(solution)/shard_map/psum | solution.py:48
  778.1 8.9 fusion.59
  831.8 39.3 %psum.127 = f32[8,1]{1,0:T(8,128)S(1)} all-reduce(f32[8,1]{1,0:T(8,128)S(1)} %copy.13), channel_id=1, replica_groups=mesh['grp'=8,'row'=4] {'grp','row'}, use_global_device_ids=true, to_apply=%region_78.0 | all-reduce | flops 8 | bytes 64 | tf_op jit(solution)/shard_map/psum | solution.py:48
  (143 shorter events, 144.9 us)
Async XLA Ops:
  7.2 93.2 %copy-start = (bf16[2,8,128,512]{3,2,1,0:T(8,128)(2,1)S(1)}, bf16[2,8,128,512]{3,2,1,0:T(8,128)(2,1)}, u32[]{:S(2)}) copy-start(bf16[2,8,128,512]{3,2,1,0:T(8,128)(2,1)} %param.35) | copy-start | bytes 6291460
  7.2 1.2 copy-start.2
  7.2 1.4 copy-start.3
  7.2 93.2 %all-gather.2.cloned.1.call-start = ((), (), s32[]{:S(2)}) async-start(), calls=%async_computation.8 | async-start | bytes 10485760 | tf_op jit(solution)/shard_map/all_gather | solution.py:31
  7.9 136.7 %reduce-scatter.9.cloned.1.call-start = ((), (), s32[]{:S(2)}) async-start(), calls=%async_computation.9 | async-start | bytes 2621440 | tf_op jit(solution)/shard_map/reduce_scatter | solution.py:46
  109.3 125.6 %reduce-scatter.11.cloned.1.call-start = ((), (), s32[]{:S(2)}) async-start(), calls=%async_computation.10 | async-start | bytes 2621440 | tf_op jit(solution)/shard_map/reduce_scatter | solution.py:46
  198.6 130.0 %reduce-scatter.13.cloned.1.call-start = ((), (), s32[]{:S(2)}) async-start(), calls=%async_computation.11 | async-start | bytes 2621440 | tf_op jit(solution)/shard_map/reduce_scatter | solution.py:46
  292.4 131.8 %reduce-scatter.15.cloned.1.call-start = ((), (), s32[]{:S(2)}) async-start(), calls=%async_computation.12 | async-start | bytes 2621440 | tf_op jit(solution)/shard_map/reduce_scatter | solution.py:46
  387.8 133.6 %reduce-scatter.17.cloned.1.call-start = ((), (), s32[]{:S(2)}) async-start(), calls=%async_computation.13 | async-start | bytes 2621440 | tf_op jit(solution)/shard_map/reduce_scatter | solution.py:46
  485.1 135.2 %reduce-scatter.19.cloned.1.call-start = ((), (), s32[]{:S(2)}) async-start(), calls=%async_computation.14 | async-start | bytes 2621440 | tf_op jit(solution)/shard_map/reduce_scatter | solution.py:46
  584.0 137.3 %reduce-scatter.21.cloned.1.call-start = ((), (), s32[]{:S(2)}) async-start(), calls=%async_computation.15 | async-start | bytes 2621440 | tf_op jit(solution)/shard_map/reduce_scatter | solution.py:46
  684.9 138.5 %reduce-scatter.23.cloned.1.call-start = ((), (), s32[]{:S(2)}) async-start(), calls=%async_computation.16 | async-start | bytes 2621440 | tf_op jit(solution)/shard_map/reduce_scatter | solution.py:46
  787.0 3.8 copy-start.8
  787.0 4.5 copy-start.7
  787.0 5.2 copy-start.6
  787.0 5.9 copy-start.5
  787.0 6.6 copy-start.4
  871.2 11.2 %copy-start.1 = (f32[8,8]{1,0:T(8,128)}, f32[8,8]{1,0:T(8,128)S(1)}, u32[]{:S(2)}) copy-start(f32[8,8]{1,0:T(8,128)S(1)} %scatter.74) | copy-start | bytes 772
Sparse Core Ops, SparseCore 0:
  9.9 90.4 all-gather.1
  109.4 35.1 reduce-scatter.8
  198.7 36.1 reduce-scatter.10
  292.5 36.1 reduce-scatter.12
  387.9 36.1 reduce-scatter.14
  485.3 36.0 reduce-scatter.16
  584.1 36.1 reduce-scatter.18
  685.0 36.2 reduce-scatter.20
  787.1 36.2 reduce-scatter.22
where the time goes:
time: 901 us; the launch traced here: 891 us
  blocking collectives  359 us (40%)
  waiting for transfers between devices  309 us (34%)
  other arithmetic  85.4 us (9%)
  matrix products  73.3 us (8%)
  local copies, waits for them, and re-layouts  39 us (4%)
  between operations  24.8 us (3%)
    psum x8, blocking collectives, local(): lax.psum((local_dots, jnp.sum(image * image)), ('grp', 'row'))  316 us
    reduce_scatter x8, waiting for transfers between devices, local(): lax.psum_scatter(partial_image, 'row', scatter_dimension=1, tiled=True)  261 us
    dot_general x8, matrix products, local(): jnp.einsum('swba,swbc->sac', left_env, inner_terms, preferred_element_typ...  70.8 us
    all_gather x1, waiting for transfers between devices, local(): right_full = lax.all_gather(right_env, 'row', axis=2, tiled=True)  47.2 us
    psum x1, blocking collectives, local(): lax.psum(jnp.sum(start_block * start_block), ('grp', 'row')) + epsilon  42.8 us
    div x7, other arithmetic, local(): krylov_basis.append(image / beta_norm)  34 us
    reduce_sum x8, other arithmetic, local(): local_dots = jnp.stack([jnp.sum(vector * image) for vector in krylov_basis])  19.7 us
  transfers between devices with their start and end apart: 9, of which 9 were waited for; matrix products, arithmetic and copies ran while one was open for 3% of the time, Pallas kernels for 0%

commit v1 on v0

--- a/solution.py
+++ b/solution.py
@@ -45,7 +45,9 @@
         )
         image = lax.psum_scatter(partial_image, "row", scatter_dimension=1, tiled=True) * live_mask
         local_dots = jnp.stack([jnp.sum(vector * image) for vector in krylov_basis])
-        coefficients, squared = lax.psum((local_dots, jnp.sum(image * image)), ("grp", "row"))
+        coefficients, squared = lax.psum(
+            lax.psum((local_dots, jnp.sum(image * image)), "row"), "grp"
+        )
         for previous in range(column + 1):
             image = image - coefficients[previous] * krylov_basis[previous]
         hessenberg = hessenberg.at[: column + 1, column].set(coefficients)

time: 901 us -> 754 us (0.84)
  blocking collectives: 359 us -> 237 us
  waiting for transfers between devices: 309 us -> 284 us
    psum x8 -> x16, blocking collectives: 316 us -> 195 us  [the longest x8 119 us: local(): lax.psum(lax.psum((local_dots, jnp.sum(image * image)), 'row'), 'grp')]
    reduce_scatter x8, waiting for transfers between devices: 261 us -> 236 us  [local(): lax.psum_scatter(partial_image, 'row', scatter_dimension=1, tiled=True)]
  transfers between devices with their start and end apart: 9 -> 9, of which waited for: 9 -> 9; matrix products, arithmetic and copies ran while one was open for 3% -> 4% of each run, Pallas kernels for 0% -> 0%
where the time goes in v1:
time: 754 us; the launch traced here: 745 us
  waiting for transfers between devices  284 us (38%)
  blocking collectives  237 us (31%)
  other arithmetic  85.6 us (11%)
  matrix products  73.3 us (10%)
  local copies, waits for them, and re-layouts  39.4 us (5%)
  between operations  24.9 us (3%)
    reduce_scatter x8, waiting for transfers between devices, local(): lax.psum_scatter(partial_image, 'row', scatter_dimension=1, tiled=True)  236 us
    psum x8, blocking collectives, local(): lax.psum(lax.psum((local_dots, jnp.sum(image * image)), 'row'), 'grp')  119 us
    psum x8, blocking collectives, local(): lax.psum((local_dots, jnp.sum(image * image)), 'row')  76 us
    dot_general x8, matrix products, local(): jnp.einsum('swba,swbc->sac', left_env, inner_terms, preferred_element_typ...  70.8 us
    all_gather x1, waiting for transfers between devices, local(): right_full = lax.all_gather(right_env, 'row', axis=2, tiled=True)  47.1 us
    psum x1, blocking collectives, local(): lax.psum(jnp.sum(start_block * start_block), ('grp', 'row')) + epsilon  42.8 us
    div x7, other arithmetic, local(): krylov_basis.append(image / beta_norm)  34 us
    reduce_sum x8, other arithmetic, local(): local_dots = jnp.stack([jnp.sum(vector * image) for vector in krylov_basis])  19.7 us
  transfers between devices with their start and end apart: 9, of which 9 were waited for; matrix products, arithmetic and copies ran while one was open for 4% of the time, Pallas kernels for 0%

profile of v1, /device:TPU:0, one launch (start us, length us, event | category | flops | bytes accessed | tf_op | source)
XLA Modules:
  0.0 745.0 jit_solution(268175293814711863)
XLA Ops:
  9.7 42.8 %psum.217 = f32[]{:T(128)} all-reduce(f32[]{:T(128)} %multiply_reduce_fusion.43), channel_id=1, replica_groups=mesh['grp'=8,'row'=4] {'grp','row'}, use_global_device_ids=true, to_apply=%region_1.0 | all-reduce | flops 1 | bytes 8 | tf_op jit(solution)/shard_map/psum | solution.py:33
  53.2 47.1 %all-gather.2.cloned.1.call-done = bf16[2,8,512,512]{3,2,1,0:T(8,128)(2,1)} async-done(((bf16[2,8,128,512]{3,2,1,0:T(8,128)(2,1)}), bf16[2,8,512,512]{3,2,1,0:T(8,128)(2,1)}) %all-gather.2.cloned.1.call-update) | async-done | bytes 8388624 | tf_op jit(solution)/shard_map/all_gather | solution.py:31
  109.3 35.3 %reduce-scatter.9.cloned.1.call-done = f32[2,128,512]{1,2,0:T(8,128)} async-done(((f32[2,512,512]{1,2,0:T(8,128)}), f32[2,128,512]{1,2,0:T(8,128)}) %reduce-scatter.9.cloned.1.call-update) | async-done | bytes 524304 | tf_op jit(solution)/shard_map/reduce_scatter | solution.py:46
  146.5 9.5 %all-reduce.14 = (f32[]{:T(128)}, f32[1]{0:T(128)}) all-reduce(f32[]{:T(128)} %get-tuple-element.226, f32[1]{0:T(128)} %bitcast.6), channel_id=1, replica_groups=mesh['grp'=8,'row'=4] {'row'}, use_global_device_ids=true, to_apply=%region_7.0 | all-reduce | flops 2 | bytes 16 | tf_op jit(solution)/shard_map/psum | solution.py:49
  156.0 14.8 %all-reduce.7 = (f32[]{:T(128)}, f32[1]{0:T(128)}) all-reduce(f32[]{:T(128)} %get-tuple-element.255, f32[1]{0:T(128)} %get-tuple-element.256), channel_id=1, replica_groups=mesh['grp'=8,'row'=4] {'grp'}, use_global_device_ids=true, to_apply=%region_8.0 | all-reduce | flops 2 | bytes 16 | tf_op jit(solution)/shard_map/psum | solution.py:48
  183.5 32.5 %reduce-scatter.11.cloned.1.call-done = f32[2,128,512]{1,2,0:T(8,128)} async-done(((f32[2,512,512]{1,2,0:T(8,128)}), f32[2,128,512]{1,2,0:T(8,128)}) %reduce-scatter.11.cloned.1.call-update) | async-done | bytes 524304 | tf_op jit(solution)/shard_map/reduce_scatter | solution.py:46
  219.2 9.5 %all-reduce.13 = (f32[]{:T(128)}, f32[2]{0:T(128)S(1)}) all-reduce(f32[]{:T(128)} %get-tuple-element.224, f32[2]{0:T(128)S(1)} %pad_maximum_fusion), channel_id=1, replica_groups=mesh['grp'=8,'row'=4] {'row'}, use_global_device_ids=true, to_apply=%region_15.0 | all-reduce | flops 3 | bytes 24 | tf_op jit(solution)/shard_map/psum | solution.py:49
  228.7 15.3 %all-reduce.6 = (f32[]{:T(128)}, f32[2]{0:T(128)S(1)}) all-reduce(f32[]{:T(128)} %get-tuple-element.253, f32[2]{0:T(128)S(1)} %get-tuple-element.254), channel_id=1, replica_groups=mesh['grp'=8,'row'=4] {'grp'}, use_global_device_ids=true, to_apply=%region_16.0 | all-reduce | flops 3 | bytes 24 | tf_op jit(solution)/shard_map/psum | solution.py:48
  258.7 32.5 %reduce-scatter.13.cloned.1.call-done = f32[2,128,512]{1,2,0:T(8,128)} async-done(((f32[2,512,512]{1,2,0:T(8,128)}), f32[2,128,512]{1,2,0:T(8,128)}) %reduce-scatter.13.cloned.1.call-update) | async-done | bytes 524304 | tf_op jit(solution)/shard_map/reduce_scatter | solution.py:46
  295.4 9.6 %all-reduce.12 = (f32[]{:T(128)}, f32[3]{0:T(128)S(1)}) all-reduce(f32[]{:T(128)} %get-tuple-element.221, f32[3]{0:T(128)S(1)} %pad_maximum_fusion.1), channel_id=1, replica_groups=mesh['grp'=8,'row'=4] {'row'}, use_global_device_ids=true, to_apply=%region_26.0 | all-reduce | flops 4 | bytes 32 | tf_op jit(solution)/shard_map/psum | solution.py:49
  305.0 14.8 %all-reduce.5 = (f32[]{:T(128)}, f32[3]{0:T(128)S(1)}) all-reduce(f32[]{:T(128)} %get-tuple-element.251, f32[3]{0:T(128)S(1)} %get-tuple-element.252), channel_id=1, replica_groups=mesh['grp'=8,'row'=4] {'grp'}, use_global_device_ids=true, to_apply=%region_27.0 | all-reduce | flops 4 | bytes 32 | tf_op jit(solution)/shard_map/psum | solution.py:48
  335.5 32.5 %reduce-scatter.15.cloned.1.call-done = f32[2,128,512]{1,2,0:T(8,128)} async-done(((f32[2,512,512]{1,2,0:T(8,128)}), f32[2,128,512]{1,2,0:T(8,128)}) %reduce-scatter.15.cloned.1.call-update) | async-done | bytes 524304 | tf_op jit(solution)/shard_map/reduce_scatter | solution.py:46
  372.9 9.6 %all-reduce.11 = (f32[]{:T(128)}, f32[4]{0:T(128)S(1)}) all-reduce(f32[]{:T(128)} %get-tuple-element.217, f32[4]{0:T(128)S(1)} %pad_maximum_fusion.2), channel_id=1, replica_groups=mesh['grp'=8,'row'=4] {'row'}, use_global_device_ids=true, to_apply=%region_38.0 | all-reduce | flops 5 | bytes 40 | tf_op jit(solution)/shard_map/psum | solution.py:49
  382.5 14.9 %all-reduce.4 = (f32[]{:T(128)}, f32[4]{0:T(128)S(1)}) all-reduce(f32[]{:T(128)} %get-tuple-element.249, f32[4]{0:T(128)S(1)} %get-tuple-element.250), channel_id=1, replica_groups=mesh['grp'=8,'row'=4] {'grp'}, use_global_device_ids=true, to_apply=%region_39.0 | all-reduce | flops 5 | bytes 40 | tf_op jit(solution)/shard_map/psum | solution.py:48
  413.9 32.5 %reduce-scatter.17.cloned.1.call-done = f32[2,128,512]{1,2,0:T(8,128)} async-done(((f32[2,512,512]{1,2,0:T(8,128)}), f32[2,128,512]{1,2,0:T(8,128)}) %reduce-scatter.17.cloned.1.call-update) | async-done | bytes 524304 | tf_op jit(solution)/shard_map/reduce_scatter | solution.py:46
  452.2 9.6 %all-reduce.10 = (f32[]{:T(128)}, f32[5]{0:T(128)S(1)}) all-reduce(f32[]{:T(128)} %get-tuple-element.211, f32[5]{0:T(128)S(1)} %stack.147), channel_id=1, replica_groups=mesh['grp'=8,'row'=4] {'row'}, use_global_device_ids=true, to_apply=%region_51.0 | all-reduce | flops 6 | bytes 48 | tf_op jit(solution)/shard_map/psum | solution.py:49
  461.8 14.8 %all-reduce.3 = (f32[]{:T(128)}, f32[5]{0:T(128)S(1)}) all-reduce(f32[]{:T(128)} %get-tuple-element.247, f32[5]{0:T(128)S(1)} %get-tuple-element.248), channel_id=1, replica_groups=mesh['grp'=8,'row'=4] {'grp'}, use_global_device_ids=true, to_apply=%region_52.0 | all-reduce | flops 6 | bytes 48 | tf_op jit(solution)/shard_map/psum | solution.py:48
  494.0 32.5 %reduce-scatter.19.cloned.1.call-done = f32[2,128,512]{1,2,0:T(8,128)} async-done(((f32[2,512,512]{1,2,0:T(8,128)}), f32[2,128,512]{1,2,0:T(8,128)}) %reduce-scatter.19.cloned.1.call-update) | async-done | bytes 524304 | tf_op jit(solution)/shard_map/reduce_scatter | solution.py:46
  533.2 9.6 %all-reduce.9 = (f32[]{:T(128)}, f32[6]{0:T(128)S(1)}) all-reduce(f32[]{:T(128)} %get-tuple-element.205, f32[6]{0:T(128)S(1)} %stack.154), channel_id=1, replica_groups=mesh['grp'=8,'row'=4] {'row'}, use_global_device_ids=true, to_apply=%region_65.0 | all-reduce | flops 7 | bytes 56 | tf_op jit(solution)/shard_map/psum | solution.py:49
  542.8 15.1 %all-reduce.2 = (f32[]{:T(128)}, f32[6]{0:T(128)S(1)}) all-reduce(f32[]{:T(128)} %get-tuple-element.245, f32[6]{0:T(128)S(1)} %get-tuple-element.246), channel_id=1, replica_groups=mesh['grp'=8,'row'=4] {'grp'}, use_global_device_ids=true, to_apply=%region_66.0 | all-reduce | flops 7 | bytes 56 | tf_op jit(solution)/shard_map/psum | solution.py:48
  576.0 32.5 %reduce-scatter.21.cloned.1.call-done = f32[2,128,512]{1,2,0:T(8,128)} async-done(((f32[2,512,512]{1,2,0:T(8,128)}), f32[2,128,512]{1,2,0:T(8,128)}) %reduce-scatter.21.cloned.1.call-update) | async-done | bytes 524304 | tf_op jit(solution)/shard_map/reduce_scatter | solution.py:46
  616.0 9.6 %all-reduce.8 = (f32[]{:T(128)}, f32[7]{0:T(128)S(1)}) all-reduce(f32[]{:T(128)} %get-tuple-element.198, f32[7]{0:T(128)S(1)} %stack.162), channel_id=1, replica_groups=mesh['grp'=8,'row'=4] {'row'}, use_global_device_ids=true, to_apply=%region_80.0 | all-reduce | flops 8 | bytes 64 | tf_op jit(solution)/shard_map/psum | solution.py:49
  625.7 14.8 %all-reduce.1 = (f32[]{:T(128)}, f32[7]{0:T(128)S(1)}) all-reduce(f32[]{:T(128)} %get-tuple-element.243, f32[7]{0:T(128)S(1)} %get-tuple-element.244), channel_id=1, replica_groups=mesh['grp'=8,'row'=4] {'grp'}, use_global_device_ids=true, to_apply=%region_81.0 | all-reduce | flops 8 | bytes 64 | tf_op jit(solution)/shard_map/psum | solution.py:48
  710.7 14.2 %psum.247 = f32[8,1]{1,0:T(8,128)S(1)} all-reduce(f32[8,1]{1,0:T(8,128)S(1)} %copy.13), channel_id=1, replica_groups=mesh['grp'=8,'row'=4] {'grp'}, use_global_device_ids=true, to_apply=%region_93.0 | all-reduce | flops 8 | bytes 64 | tf_op jit(solution)/shard_map/psum | solution.py:48
  (151 shorter events, 214.1 us)
Async XLA Ops:
  7.2 93.2 %copy-start = (bf16[2,8,128,512]{3,2,1,0:T(8,128)(2,1)S(1)}, bf16[2,8,128,512]{3,2,1,0:T(8,128)(2,1)}, u32[]{:S(2)}) copy-start(bf16[2,8,128,512]{3,2,1,0:T(8,128)(2,1)} %param.35) | copy-start | bytes 6291460
  7.2 1.2 copy-start.2
  7.2 1.4 copy-start.3
  7.2 93.2 %all-gather.2.cloned.1.call-start = ((), (), s32[]{:S(2)}) async-start(), calls=%async_computation.8 | async-start | bytes 10485760 | tf_op jit(solution)/shard_map/all_gather | solution.py:31
  7.9 136.7 %reduce-scatter.9.cloned.1.call-start = ((), (), s32[]{:S(2)}) async-start(), calls=%async_computation.9 | async-start | bytes 2621440 | tf_op jit(solution)/shard_map/reduce_scatter | solution.py:46
  109.3 106.7 %reduce-scatter.11.cloned.1.call-start = ((), (), s32[]{:S(2)}) async-start(), calls=%async_computation.10 | async-start | bytes 2621440 | tf_op jit(solution)/shard_map/reduce_scatter | solution.py:46
  183.4 107.8 %reduce-scatter.13.cloned.1.call-start = ((), (), s32[]{:S(2)}) async-start(), calls=%async_computation.11 | async-start | bytes 2621440 | tf_op jit(solution)/shard_map/reduce_scatter | solution.py:46
  258.7 109.3 %reduce-scatter.15.cloned.1.call-start = ((), (), s32[]{:S(2)}) async-start(), calls=%async_computation.12 | async-start | bytes 2621440 | tf_op jit(solution)/shard_map/reduce_scatter | solution.py:46
  335.4 111.0 %reduce-scatter.17.cloned.1.call-start = ((), (), s32[]{:S(2)}) async-start(), calls=%async_computation.13 | async-start | bytes 2621440 | tf_op jit(solution)/shard_map/reduce_scatter | solution.py:46
  413.9 112.7 %reduce-scatter.19.cloned.1.call-start = ((), (), s32[]{:S(2)}) async-start(), calls=%async_computation.14 | async-start | bytes 2621440 | tf_op jit(solution)/shard_map/reduce_scatter | solution.py:46
  494.0 114.6 %reduce-scatter.21.cloned.1.call-start = ((), (), s32[]{:S(2)}) async-start(), calls=%async_computation.15 | async-start | bytes 2621440 | tf_op jit(solution)/shard_map/reduce_scatter | solution.py:46
  576.0 115.9 %reduce-scatter.23.cloned.1.call-start = ((), (), s32[]{:S(2)}) async-start(), calls=%async_computation.16 | async-start | bytes 2621440 | tf_op jit(solution)/shard_map/reduce_scatter | solution.py:46
  659.3 3.8 copy-start.8
  659.3 4.5 copy-start.7
  659.3 5.2 copy-start.6
  659.3 5.9 copy-start.5
  659.3 6.6 copy-start.4
  725.0 11.2 %copy-start.1 = (f32[8,8]{1,0:T(8,128)}, f32[8,8]{1,0:T(8,128)S(1)}, u32[]{:S(2)}) copy-start(f32[8,8]{1,0:T(8,128)S(1)} %scatter.74) | copy-start | bytes 772
Sparse Core Ops, SparseCore 0:
  9.9 90.4 all-gather.1
  109.4 35.1 reduce-scatter.8
  183.5 32.3 reduce-scatter.10
  258.8 32.3 reduce-scatter.12
  335.5 32.3 reduce-scatter.14
  414.0 32.3 reduce-scatter.16
  494.1 32.3 reduce-scatter.18
  576.1 32.3 reduce-scatter.20
  659.5 32.3 reduce-scatter.22
